TPU v7x, 512 devices: a whole 4x8x8 slice. The times are simulated.
512 devices in a mesh: wide: 64 (over z, y_hi, core), narrow: 8 (over x, y_lo).
Axes of the slice: x: 4, y: 8 (y_hi: 4, y_lo: 2; y = y_hi * 2 + y_lo), z: 8, core: 2. Of those that a mesh axis runs over, the one named last changes fastest.
Arguments:
- hidden_in: bfloat16 [16384, 2048], P('wide', 'narrow'), may hold values from -64 to 64
- cache_lengths: int32 [128], P('wide'), may hold values from 1 to 1023, as said below
- cache_offsets: int32 [128], P('wide'), may hold values from 0 to 65535, as said below
- cache_kv: bfloat16 [2, 2, 65536, 2048], P(None, None, 'wide', 'narrow'), may hold values from -16 to 16
- w_qkv: bfloat16 [2048, 3, 2048], P('wide', None, 'narrow'), may hold values from -0.125 to 0.125
- qkv_bias: bfloat16 [3, 2048], P(None, 'narrow'), may hold values from -40 to 40
- w_out: bfloat16 [2048, 2048], P('wide', 'narrow'), may hold values from -0.125 to 0.125
- out_bias: bfloat16 [2048], P('narrow'), may hold values from -3 to 3
- norm_gain: bfloat16 [2048], P('narrow'), may hold values from 0.2 to 5
- norm_shift: bfloat16 [2048], P('narrow'), may hold values from -3 to 3
Outputs:
- hidden_out: bfloat16 [16384, 2048], P('wide', 'narrow')
- new_cache: bfloat16 [2, 2, 16384, 2048], P(None, None, 'wide', 'narrow')
Inputs may be any that keep to these rules, and one draw needn't show every extreme that they name: `cache_lengths`: the cached lengths of the 2 requests r with the same r // 2 sum to at most 1024; for some such group exactly 1024, and in it one request has 1023 rows. Request r's cache is rows cache_offsets[r] to cache_offsets[r] + cache_lengths[r] - 1 of the packed cache, all within rows (r // 2) * 1024 to (r // 2 + 1) * 1024 - 1; the row ranges of different requests are disjoint.
All inputs are finite; a program needn't handle non-finite values.
Results may differ from a plain program's by a relative error of at most 0.02.
Values may be sent and summed in bfloat16 or wider, within the bound.
No kernel may reach another device: no remote copies, remote signals or barrier semaphores. Data moves between devices by JAX's collectives and lax.ppermute only.
A program may use at most 64 MiB of HBM per device.

v0:
```python
import math
import jax
import jax.numpy as jnp
from jax import lax
from jax.sharding import PartitionSpec as P

HEAD = 128
SPAN = 128
LAYERS = 2
EPSILON = 1e-05
NEGATIVE = -1e30


def add_rows(shard_piece, operand):
    piece_rows = shard_piece.shape[0]
    return jnp.dot(operand, shard_piece.reshape(piece_rows, -1), preferred_element_type=jnp.float32)


def norm_slice(summed, norm_gain, norm_shift, full_width):
    values = summed.astype(jnp.float32)
    row_means = lax.psum(jnp.sum(values, axis=1), "narrow") / full_width
    centered = values - row_means[:, None]
    row_spread = lax.psum(jnp.sum(centered * centered, axis=1), "narrow") / full_width
    scaled = centered * lax.rsqrt(row_spread[:, None] + EPSILON)
    return (scaled * norm_gain.astype(jnp.float32) + norm_shift.astype(jnp.float32)).astype(
        jnp.bfloat16
    )


def attend(queries, keys_new, values_new, keys_cache, values_cache, live_cache, live_new):
    scale_factor = 1.0 / math.sqrt(queries.shape[2])
    scores_cache = (
        jnp.einsum("qhd,khd->hqk", queries, keys_cache, preferred_element_type=jnp.float32)
        * scale_factor
    )
    scores_new = (
        jnp.einsum("qhd,khd->hqk", queries, keys_new, preferred_element_type=jnp.float32)
        * scale_factor
    )
    masked_cache = jnp.where(live_cache[None], scores_cache, NEGATIVE)
    masked_new = jnp.where(live_new[None], scores_new, NEGATIVE)
    top_score = jnp.maximum(jnp.max(masked_cache, axis=2), jnp.max(masked_new, axis=2))[:, :, None]
    weights_cache = jnp.where(live_cache[None], jnp.exp(masked_cache - top_score), 0.0)
    weights_new = jnp.where(live_new[None], jnp.exp(masked_new - top_score), 0.0)
    totals = jnp.sum(weights_cache, axis=2, keepdims=True) + jnp.sum(
        weights_new, axis=2, keepdims=True
    )
    probs_cache = (weights_cache / totals).astype(jnp.bfloat16)
    probs_new = (weights_new / totals).astype(jnp.bfloat16)
    combined = jnp.einsum(
        "hqk,khd->qhd", probs_cache, values_cache, preferred_element_type=jnp.float32
    )
    combined = combined + jnp.einsum(
        "hqk,khd->qhd", probs_new, values_new, preferred_element_type=jnp.float32
    )
    return combined.astype(jnp.bfloat16).reshape(queries.shape[0], -1)


def shards(
    hidden_in,
    cache_lengths,
    cache_offsets,
    cache_kv,
    w_qkv,
    qkv_bias,
    w_out,
    out_bias,
    norm_gain,
    norm_shift,
):
    row_count, local_width = hidden_in.shape
    full_width = local_width * lax.axis_size("narrow")
    local_heads = local_width // HEAD
    cache_count = cache_kv.shape[2]
    requests_here = cache_lengths.shape[0]
    block_start = lax.axis_index("wide") * cache_count
    rows_global = block_start + jnp.arange(cache_count, dtype=jnp.int32)
    row_start = jnp.broadcast_to(cache_offsets[:, None], (requests_here, SPAN)).reshape(-1)
    row_stop = row_start + jnp.broadcast_to(cache_lengths[:, None], (requests_here, SPAN)).reshape(
        -1
    )
    live_cache = (rows_global[None, :] >= row_start[:, None]) & (
        rows_global[None, :] < row_stop[:, None]
    )
    owner_index = jnp.arange(row_count, dtype=jnp.int32) // SPAN
    position = jnp.arange(row_count, dtype=jnp.int32) % SPAN
    live_new = (owner_index[:, None] == owner_index[None, :]) & (
        position[:, None] >= position[None, :]
    )
    bias_flat = qkv_bias.astype(jnp.float32).reshape(-1)
    gathered = lax.all_gather(hidden_in, "narrow", axis=1, tiled=True)
    carried = hidden_in
    appended = []
    for layer_index in range(LAYERS):
        projections = add_rows(lax.all_gather(w_qkv, "wide", axis=0, tiled=True), operand=gathered)
        projections = projections + bias_flat
        queries = projections[:, :local_width].astype(jnp.bfloat16)
        keys_new = projections[:, local_width : 2 * local_width].astype(jnp.bfloat16)
        values_new = projections[:, 2 * local_width :].astype(jnp.bfloat16)
        appended.append(jnp.stack([keys_new, values_new]))
        keys_cache = cache_kv[layer_index, 0].reshape(cache_count, local_heads, HEAD)
        values_cache = cache_kv[layer_index, 1].reshape(cache_count, local_heads, HEAD)
        attended = attend(
            queries.reshape(row_count, local_heads, HEAD),
            keys_new.reshape(row_count, local_heads, HEAD),
            values_new.reshape(row_count, local_heads, HEAD),
            keys_cache,
            values_cache,
            live_cache,
            live_new,
        )
        heads_all = lax.all_gather(attended, "narrow", axis=1, tiled=True)
        projected = add_rows(lax.all_gather(w_out, "wide", axis=0, tiled=True), operand=heads_all)
        summed = (projected + out_bias.astype(jnp.float32) + carried.astype(jnp.float32)).astype(
            jnp.bfloat16
        )
        if layer_index + 1 < LAYERS:
            carried = norm_slice(summed, norm_gain, norm_shift, full_width)
            gathered = lax.all_gather(carried, "narrow", axis=1, tiled=True)
        else:
            carried = norm_slice(summed, norm_gain, norm_shift, full_width)
    return (carried, jnp.stack(appended))


def solution(mesh):
    in_specs = (
        P("wide", "narrow"),
        P("wide"),
        P("wide"),
        P(None, None, "wide", "narrow"),
        P("wide", None, "narrow"),
        P(None, "narrow"),
        P("wide", "narrow"),
        P("narrow"),
        P("narrow"),
        P("narrow"),
    )
    out_specs = (P("wide", "narrow"), P(None, None, "wide", "narrow"))
    return jax.shard_map(shards, mesh=mesh, in_specs=in_specs, out_specs=out_specs, check_vma=False)
```

profile of v0, /device:TPU:40, one launch (start us, length us, event | category | flops | bytes accessed | tf_op | source)
XLA Modules:
  0.0 457.5 jit_solution(16025079761975126802)
XLA Ops:
  11.6 2.6 fusion.54
  14.2 1.0 copy.70
  15.3 1.0 copy.51
  16.7 83.8 %all-gather.9.cloned.1.call-done = bf16[2048,3,256]{2,0,1:T(8,128)(2,1)} async-done(((bf16[32,3,256]{2,0,1:T(8,128)(2,1)}), bf16[2048,3,256]{2,0,1:T(8,128)(2,1)}) %all-gather.9.cloned.1.call-update) | async-done | bytes 3145744 | tf_op jit(solution)/shard_map/all_gather | solution.py:95
  100.5 3.2 copy.45
  103.7 41.0 %all-gather.7.cloned.1.call-done = bf16[256,2048]{1,0:T(8,128)(2,1)} async-done(((bf16[256,256]{1,0:T(8,128)(2,1)}), bf16[256,2048]{1,0:T(8,128)(2,1)}) %all-gather.7.cloned.1.call-update) | async-done | bytes 1048592 | tf_op jit(solution)/shard_map/all_gather | solution.py:91
  144.7 2.2 fusion.4
  146.9 0.8 slice_bitcast_fusion.4
  147.7 1.7 copy.68
  149.4 1.2 fusion.55
  150.6 1.8 fusion
  153.4 0.8 convolution_bitcast_fusion.3
  154.3 0.9 fusion.16
  155.3 1.7 copy.54
  157.0 73.5 %all-gather.13.cloned.1.call-done = bf16[2048,256]{1,0:T(8,128)(2,1)} async-done(((bf16[32,256]{1,0:T(8,128)(2,1)}), bf16[2048,256]{1,0:T(8,128)(2,1)}) %all-gather.13.cloned.1.call-update) | async-done | bytes 1048592 | tf_op jit(solution)/shard_map/all_gather | solution.py:113
  230.5 43.9 %all-gather.11.cloned.1.call-done = bf16[256,2048]{0,1:T(8,128)(2,1)} async-done(((bf16[256,256]{0,1:T(8,128)(2,1)}), bf16[256,2048]{0,1:T(8,128)(2,1)}) %all-gather.11.cloned.1.call-update) | async-done | bytes 1048592 | tf_op jit(solution)/shard_map/all_gather | solution.py:112
  274.4 2.8 fusion.56
  277.2 18.7 %psum.28 = f32[256]{0:T(256)S(1)} all-reduce(f32[256]{0:T(256)S(1)} %get-tuple-element.26), channel_id=1, replica_groups=mesh['wide'=64,'narrow'=8] {'narrow'}, use_global_device_ids=true, to_apply=%region_5.6 | all-reduce | flops 256 | bytes 2048 | tf_op jit(solution)/shard_map/psum | solution.py:21
  295.9 1.0 multiply_reduce_fusion.1
  296.9 17.6 %psum.29 = f32[256]{0:T(256)S(1)} all-reduce(f32[256]{0:T(256)S(1)} %multiply_reduce_fusion.1), channel_id=1, replica_groups=mesh['wide'=64,'narrow'=8] {'narrow'}, use_global_device_ids=true, to_apply=%region_7.8 | all-reduce | flops 256 | bytes 2048 | tf_op jit(solution)/shard_map/psum | solution.py:23
  314.5 1.7 add_convert_fusion.1
  316.3 2.0 copy.71
  318.3 2.0 copy.60
  320.4 37.9 %all-gather.15.cloned.1.call-done = bf16[256,2048]{0,1:T(8,128)(2,1)} async-done(((bf16[256,256]{0,1:T(8,128)(2,1)}), bf16[256,2048]{0,1:T(8,128)(2,1)}) %all-gather.15.cloned.1.call-update) | async-done | bytes 1048592 | tf_op jit(solution)/shard_map/all_gather | solution.py:119
  358.2 2.3 fusion.5
  363.2 1.7 copy.69
  365.7 0.9 fusion.17
  366.8 0.8 pad_maximum_fusion
  367.6 43.9 %all-gather.17.cloned.1.call-done = bf16[256,2048]{0,1:T(8,128)(2,1)} async-done(((bf16[256,256]{0,1:T(8,128)(2,1)}), bf16[256,2048]{0,1:T(8,128)(2,1)}) %all-gather.17.cloned.1.call-update) | async-done | bytes 1048592 | tf_op jit(solution)/shard_map/all_gather | solution.py:112
  411.5 1.8 fusion.58
  413.4 18.7 %psum.30 = f32[256]{0:T(256)S(1)} all-reduce(f32[256]{0:T(256)S(1)} %get-tuple-element.32), channel_id=1, replica_groups=mesh['wide'=64,'narrow'=8] {'narrow'}, use_global_device_ids=true, to_apply=%region_13.14 | all-reduce | flops 256 | bytes 2048 | tf_op jit(solution)/shard_map/psum | solution.py:21
  432.1 17.6 %psum.31 = f32[256]{0:T(256)S(1)} all-reduce(f32[256]{0:T(256)S(1)} %multiply_reduce_fusion), channel_id=1, replica_groups=mesh['wide'=64,'narrow'=8] {'narrow'}, use_global_device_ids=true, to_apply=%region_15.16 | all-reduce | flops 256 | bytes 2048 | tf_op jit(solution)/shard_map/psum | solution.py:23
  (71 shorter events, 10.5 us)
Async XLA Ops:
  7.2 93.3 %all-gather.9.cloned.1.call-start = ((), (), s32[]{:S(2)}) async-start(), calls=%async_computation.1 | async-start | bytes 3194880 | tf_op jit(solution)/shard_map/all_gather | solution.py:95
  7.9 136.8 %all-gather.7.cloned.1.call-start = ((), (), s32[]{:S(2)}) async-start(), calls=%async_computation | async-start | bytes 1179648 | tf_op jit(solution)/shard_map/all_gather | solution.py:91
  8.6 221.9 %all-gather.13.cloned.1.call-start = ((), (), s32[]{:S(2)}) async-start(), calls=%async_computation.3 | async-start | bytes 1064960 | tf_op jit(solution)/shard_map/all_gather | solution.py:113
  9.4 265.0 %all-gather.11.cloned.1.call-start = ((), (), s32[]{:S(2)}) async-start(), calls=%async_computation.2 | async-start | bytes 1179648 | tf_op jit(solution)/shard_map/all_gather | solution.py:112
  152.4 1.0 copy-start.2
  153.4 0.9 copy-start.8
  154.3 2.7 copy-start.11
  154.3 2.7 copy-start.12
  154.3 2.7 copy-start.13
  155.3 202.9 %all-gather.15.cloned.1.call-start = ((), (), s32[]{:S(2)}) async-start(), calls=%async_computation.4 | async-start | bytes 1179648 | tf_op jit(solution)/shard_map/all_gather | solution.py:119
  316.2 95.3 %all-gather.17.cloned.1.call-start = ((), (), s32[]{:S(2)}) async-start(), calls=%async_computation.5 | async-start | bytes 1179648 | tf_op jit(solution)/shard_map/all_gather | solution.py:112
  358.2 3.3 copy-start
  362.2 2.6 copy-start.3
  364.8 0.9 copy-start.9
  365.7 1.0 copy-start.4
  365.7 1.0 copy-start.5
  365.7 1.1 copy-start.6
  365.7 1.1 copy-start.7
  365.7 45.8 %copy-start.1 = (bf16[256,256]{0,1:T(8,128)(2,1)S(1)}, bf16[256,256]{0,1:T(8,128)(2,1)}, u32[]{:S(2)}) copy-start(bf16[256,256]{0,1:T(8,128)(2,1)} %add_convert_fusion.1) | copy-start | bytes 393220
  365.7 45.8 %copy-start.10 = (bf16[2048,256]{1,0:T(8,128)(2,1)S(1)}, bf16[2048,256]{1,0:T(8,128)(2,1)}, u32[]{:S(2)}) copy-start(bf16[2048,256]{1,0:T(8,128)(2,1)} %all-gather.13.cloned.1.call-done) | copy-start | bytes 3145732
Sparse Core Ops, SparseCore 0:
  11.4 89.0 all-gather.8
  102.5 42.1 all-gather.6
  148.0 82.4 all-gather.12
  232.4 41.8 all-gather.10
  316.3 41.8 all-gather.14
  366.8 44.6 all-gather.16
where the time goes:
time: 458 us; the launch traced here: 457 us
  waiting for transfers between devices  326 us (71%)
  blocking collectives  72.6 us (16%)
  local copies, waits for them, and re-layouts  20.9 us (5%)
  matrix products  16.5 us (4%)
  between operations  14.4 us (3%)
  other arithmetic  6.96 us (2%)
    all_gather x2, waiting for transfers between devices, shards(): heads_all = lax.all_gather(attended, 'narrow', axis=1, tiled=True)  87.8 us
    all_gather x1, waiting for transfers between devices, shards(): lax.all_gather(w_qkv, 'wide', axis=0, tiled=True)  83.8 us
    all_gather x1, waiting for transfers between devices, shards(): lax.all_gather(w_out, 'wide', axis=0, tiled=True)  73.5 us
    all_gather x1, waiting for transfers between devices, shards(): gathered = lax.all_gather(hidden_in, 'narrow', axis=1, tiled=True)  41 us
    all_gather x1, waiting for transfers between devices, shards(): gathered = lax.all_gather(carried, 'narrow', axis=1, tiled=True)  37.9 us
    psum x2, blocking collectives, norm_slice(): row_means = lax.psum(jnp.sum(values, axis=1), 'narrow') / full_width  37.4 us
    psum x2, blocking collectives, norm_slice(): lax.psum(jnp.sum(centered * centered, axis=1), 'narrow') / full_width  35.2 us
  transfers between devices with their start and end apart: 6, of which 6 were waited for; matrix products, arithmetic and copies ran while one was open for 6% of the time, Pallas kernels for 0%

commit v1 on v0

--- a/solution.py
+++ b/solution.py
@@ -88,7 +88,10 @@
         position[:, None] >= position[None, :]
     )
     bias_flat = qkv_bias.astype(jnp.float32).reshape(-1)
-    gathered = lax.all_gather(hidden_in, "narrow", axis=1, tiled=True)
+    n_dev = lax.axis_size("narrow")
+    tiles = jnp.stack([hidden_in for _ in range(n_dev)])
+    tiles = lax.all_to_all(tiles, "narrow", split_axis=0, concat_axis=0)
+    gathered = jnp.concatenate(tiles, axis=1)
     carried = hidden_in
     appended = []
     for layer_index in range(LAYERS):

time: 458 us -> 410 us (0.90)
  waiting for transfers between devices: 326 us -> 275 us
  starting transfers between devices: 0.24 us -> 5.92 us
    all_gather x1 -> x0, waiting for transfers between devices: 41 us -> none  [shards(): gathered = lax.all_gather(hidden_in, 'narrow', axis=1, tiled=True)]
    all_to_all x0 -> x1, starting transfers between devices: none -> 5.76 us  [shards(): tiles = lax.all_to_all(tiles, 'narrow', split_axis=0, concat_axis=0)]
    all_gather x1, waiting for transfers between devices: 73.5 us -> 67.9 us  [shards(): lax.all_gather(w_out, 'wide', axis=0, tiled=True)]
  transfers between devices with their start and end apart: 6 -> 6, of which waited for: 6 -> 5; matrix products, arithmetic and copies ran while one was open for 6% -> 6% of each run, Pallas kernels for 0% -> 0%
where the time goes in v1:
time: 410 us; the launch traced here: 409 us
  waiting for transfers between devices  275 us (67%)
  blocking collectives  72.6 us (18%)
  local copies, waits for them, and re-layouts  18.5 us (5%)
  matrix products  16.6 us (4%)
  between operations  14.1 us (3%)
  other arithmetic  6.3 us (2%)
  starting transfers between devices  5.92 us (1%)
    all_gather x2, waiting for transfers between devices, shards(): heads_all = lax.all_gather(attended, 'narrow', axis=1, tiled=True)  87.9 us
    all_gather x1, waiting for transfers between devices, shards(): lax.all_gather(w_qkv, 'wide', axis=0, tiled=True)  80.2 us
    all_gather x1, waiting for transfers between devices, shards(): lax.all_gather(w_out, 'wide', axis=0, tiled=True)  67.9 us
    all_gather x1, waiting for transfers between devices, shards(): gathered = lax.all_gather(carried, 'narrow', axis=1, tiled=True)  37.8 us
    psum x2, blocking collectives, norm_slice(): row_means = lax.psum(jnp.sum(values, axis=1), 'narrow') / full_width  37.4 us
    psum x2, blocking collectives, norm_slice(): lax.psum(jnp.sum(centered * centered, axis=1), 'narrow') / full_width  35.2 us
    dot_general x4, matrix products, add_rows(): jnp.dot(operand, shard_piece.reshape(piece_rows, -1), preferred_element_t...  9.2 us
  transfers between devices with their start and end apart: 6, of which 5 were waited for; matrix products, arithmetic and copies ran while one was open for 6% of the time, Pallas kernels for 0%

profile of v1, /device:TPU:40, one launch (start us, length us, event | category | flops | bytes accessed | tf_op | source)
XLA Modules:
  0.0 409.2 jit_solution(4333898268683796038)
XLA Ops:
  7.9 1.0 copy.46
  8.9 1.1 stack.38
  10.0 5.8 %all-to-all-start = ((bf16[8,256,256]{1,2,0:T(8,128)(2,1)}), bf16[8,256,256]{1,2,0:T(8,128)(2,1)}, u32[]{:S(2)}, u32[]{:S(2)}) async-start(bf16[8,256,256]{1,2,0:T(8,128)(2,1)} %stack.38), calls=%async_computation | async-start | bytes 2097152 | tf_op jit(solution)/shard_map/all_to_all | solution.py:93
  16.6 1.1 fusion.54
  17.7 1.0 copy.72
  18.7 1.0 copy.53
  20.3 80.2 %all-gather.6.cloned.1.call-done = bf16[2048,3,256]{2,0,1:T(8,128)(2,1)} async-done(((bf16[32,3,256]{2,0,1:T(8,128)(2,1)}), bf16[2048,3,256]{2,0,1:T(8,128)(2,1)}) %all-gather.6.cloned.1.call-update) | async-done | bytes 3145744 | tf_op jit(solution)/shard_map/all_gather | solution.py:98
  100.5 3.2 copy.47
  103.7 2.3 fusion.4
  106.0 0.9 slice_bitcast_fusion.4
  106.8 1.7 copy.70
  108.5 1.2 fusion.55
  109.7 1.8 fusion
  112.5 0.8 convolution_bitcast_fusion.3
  113.4 0.9 fusion.16
  114.5 67.9 %all-gather.10.cloned.1.call-done = bf16[2048,256]{1,0:T(8,128)(2,1)} async-done(((bf16[32,256]{1,0:T(8,128)(2,1)}), bf16[2048,256]{1,0:T(8,128)(2,1)}) %all-gather.10.cloned.1.call-update) | async-done | bytes 1048592 | tf_op jit(solution)/shard_map/all_gather | solution.py:116
  182.4 44.0 %all-gather.8.cloned.1.call-done = bf16[256,2048]{0,1:T(8,128)(2,1)} async-done(((bf16[256,256]{0,1:T(8,128)(2,1)}), bf16[256,2048]{0,1:T(8,128)(2,1)}) %all-gather.8.cloned.1.call-update) | async-done | bytes 1048592 | tf_op jit(solution)/shard_map/all_gather | solution.py:115
  226.4 2.8 fusion.56
  229.2 18.7 %psum.28 = f32[256]{0:T(256)S(1)} all-reduce(f32[256]{0:T(256)S(1)} %get-tuple-element.26), channel_id=1, replica_groups=mesh['wide'=64,'narrow'=8] {'narrow'}, use_global_device_ids=true, to_apply=%region_5.6 | all-reduce | flops 256 | bytes 2048 | tf_op jit(solution)/shard_map/psum | solution.py:21
  247.9 1.0 multiply_reduce_fusion.1
  248.9 17.6 %psum.29 = f32[256]{0:T(256)S(1)} all-reduce(f32[256]{0:T(256)S(1)} %multiply_reduce_fusion.1), channel_id=1, replica_groups=mesh['wide'=64,'narrow'=8] {'narrow'}, use_global_device_ids=true, to_apply=%region_7.8 | all-reduce | flops 256 | bytes 2048 | tf_op jit(solution)/shard_map/psum | solution.py:23
  266.5 1.7 add_convert_fusion.1
  268.3 2.1 copy.73
  270.4 2.0 copy.62
  272.5 37.8 %all-gather.12.cloned.1.call-done = bf16[256,2048]{0,1:T(8,128)(2,1)} async-done(((bf16[256,256]{0,1:T(8,128)(2,1)}), bf16[256,2048]{0,1:T(8,128)(2,1)}) %all-gather.12.cloned.1.call-update) | async-done | bytes 1048592 | tf_op jit(solution)/shard_map/all_gather | solution.py:122
  310.3 2.3 fusion.5
  315.2 1.7 copy.71
  317.8 0.9 fusion.17
  319.7 43.9 %all-gather.14.cloned.1.call-done = bf16[256,2048]{0,1:T(8,128)(2,1)} async-done(((bf16[256,256]{0,1:T(8,128)(2,1)}), bf16[256,2048]{0,1:T(8,128)(2,1)}) %all-gather.14.cloned.1.call-update) | async-done | bytes 1048592 | tf_op jit(solution)/shard_map/all_gather | solution.py:115
  363.6 1.8 fusion.58
  365.4 18.7 %psum.30 = f32[256]{0:T(256)S(1)} all-reduce(f32[256]{0:T(256)S(1)} %get-tuple-element.32), channel_id=1, replica_groups=mesh['wide'=64,'narrow'=8] {'narrow'}, use_global_device_ids=true, to_apply=%region_13.14 | all-reduce | flops 256 | bytes 2048 | tf_op jit(solution)/shard_map/psum | solution.py:21
  384.2 17.6 %psum.31 = f32[256]{0:T(256)S(1)} all-reduce(f32[256]{0:T(256)S(1)} %multiply_reduce_fusion), channel_id=1, replica_groups=mesh['wide'=64,'narrow'=8] {'narrow'}, use_global_device_ids=true, to_apply=%region_15.16 | all-reduce | flops 256 | bytes 2048 | tf_op jit(solution)/shard_map/psum | solution.py:23
  (81 shorter events, 8.7 us)
Async XLA Ops:
  7.2 9.4 %copy-start.12 = (bf16[3,256]{1,0:T(4,128)(2,1)S(1)}, bf16[3,256]{1,0:T(4,128)(2,1)}, u32[]{:S(2)}) copy-start(bf16[3,256]{1,0:T(4,128)(2,1)} %param.15) | copy-start | bytes 4612
  7.2 9.4 %copy-start.1 = (bf16[2,2,1024,256]{3,2,1,0:T(8,128)(2,1)S(1)}, bf16[2,2,1024,256]{3,2,1,0:T(8,128)(2,1)}, u32[]{:S(2)}) copy-start(bf16[2,2,1024,256]{3,2,1,0:T(8,128)(2,1)} %param.13) | copy-start | bytes 6291460
  7.2 93.3 %all-gather.6.cloned.1.call-start = ((), (), s32[]{:S(2)}) async-start(), calls=%async_computation.1 | async-start | bytes 3194880 | tf_op jit(solution)/shard_map/all_gather | solution.py:98
  8.9 7.7 %copy-start.2 = (bf16[256,256]{0,1:T(8,128)(2,1)}, bf16[256,256]{0,1:T(8,128)(2,1)S(1)}, u32[]{:S(2)}) copy-start(bf16[256,256]{0,1:T(8,128)(2,1)S(1)} %copy.46) | copy-start | bytes 393220
  10.0 93.7 %all-to-all-start = ((bf16[8,256,256]{1,2,0:T(8,128)(2,1)}), bf16[8,256,256]{1,2,0:T(8,128)(2,1)}, u32[]{:S(2)}, u32[]{:S(2)}) async-start(bf16[8,256,256]{1,2,0:T(8,128)(2,1)} %stack.38), calls=%async_computation | async-start | bytes 2097152 | tf_op jit(solution)/shard_map/all_to_all | solution.py:93
  15.8 166.6 %all-gather.10.cloned.1.call-start = ((), (), s32[]{:S(2)}) async-start(), calls=%async_computation.3 | async-start | bytes 1064960 | tf_op jit(solution)/shard_map/all_gather | solution.py:116
  16.5 209.9 %all-gather.8.cloned.1.call-start = ((), (), s32[]{:S(2)}) async-start(), calls=%async_computation.2 | async-start | bytes 1179648 | tf_op jit(solution)/shard_map/all_gather | solution.py:115
  17.7 2.0 copy-start.14
  17.7 2.1 copy-start.13
  111.5 1.0 copy-start.4
  112.5 0.9 copy-start.10
  113.4 1.1 copy-start.16
  113.4 1.1 copy-start.17
  113.4 1.1 copy-start.18
  114.4 195.9 %all-gather.12.cloned.1.call-start = ((), (), s32[]{:S(2)}) async-start(), calls=%async_computation.4 | async-start | bytes 1179648 | tf_op jit(solution)/shard_map/all_gather | solution.py:122
  268.3 95.3 %all-gather.14.cloned.1.call-start = ((), (), s32[]{:S(2)}) async-start(), calls=%async_computation.5 | async-start | bytes 1179648 | tf_op jit(solution)/shard_map/all_gather | solution.py:115
  310.3 3.3 copy-start
  314.3 2.6 copy-start.5
  316.9 0.9 copy-start.11
  317.7 1.0 copy-start.6
  317.7 1.0 copy-start.7
  317.7 1.1 copy-start.8
  317.8 1.1 copy-start.9
  317.8 45.8 %copy-start.3 = (bf16[256,256]{0,1:T(8,128)(2,1)S(1)}, bf16[256,256]{0,1:T(8,128)(2,1)}, u32[]{:S(2)}) copy-start(bf16[256,256]{0,1:T(8,128)(2,1)} %add_convert_fusion.1) | copy-start | bytes 393220
  317.8 45.8 %copy-start.15 = (bf16[2048,256]{1,0:T(8,128)(2,1)S(1)}, bf16[2048,256]{1,0:T(8,128)(2,1)}, u32[]{:S(2)}) copy-start(bf16[2048,256]{1,0:T(8,128)(2,1)} %all-gather.10.cloned.1.call-done) | copy-start | bytes 3145732
Sparse Core Ops, SparseCore 0:
  11.4 89.0 all-gather.5
  103.9 78.4 all-gather.9
  184.5 41.8 all-gather.7
  268.4 41.8 all-gather.11
  318.9 44.6 all-gather.13
